TPU v7x, 32 devices: a whole 2x2x4 slice. The times are simulated.
32 devices in a mesh: blk: 8 (over z, y), grp: 4 (over x, core).
Axes of the slice: x: 2, y: 2, z: 4, core: 2. Of those that a mesh axis runs over, the one named last changes fastest.
Arguments:
- embeddings: bfloat16 [4, 4096, 1024], P('grp', 'blk'), may hold values from -12 to 12
- strata: int32 [4, 4096], P('grp', 'blk'), may hold values from 0 to 127, as said below
- centroids: bfloat16 [4, 128, 1024], P('grp', 'blk'), may hold values from -12 to 12
Outputs:
- probs: float32 [4, 4096], P('grp', 'blk')
Inputs may be any that keep to these rules, and one draw needn't show every extreme that they name: `strata`: within each aligned run of 512 rows of a collection the stratum ids never fall; within each range of 16 consecutive ids the smallest are about four times as common as the largest. `strata`: in each aligned run of 512 rows, at most 128 rows have ids in one range k * 16 to (k + 1) * 16 - 1, and exactly 128 in some range.
All inputs are finite; a program needn't handle non-finite values.
Results may differ from a plain program's by a relative error of at most 0.0014.
Values may be sent and summed in bfloat16 or wider, within the bound.
No kernel may reach another device: no remote copies, remote signals or barrier semaphores. Data moves between devices by JAX's collectives and lax.ppermute only.
A program may use at most 64 MiB of HBM per device.

v0:
```python
import math
import jax
import jax.numpy as jnp
from jax import lax
from jax.sharding import PartitionSpec as P

sharpness_divisor = 0.25
base_term = 0.05
epsilon = 1e-06


def unit_rows(matrix):
    values = matrix.astype(jnp.float32)
    scaling = lax.rsqrt(jnp.mean(values * values, axis=-1, keepdims=True) + epsilon) / math.sqrt(
        matrix.shape[-1]
    )
    return (values * scaling).astype(jnp.bfloat16)


def dense_sums(query_rows, query_ids, key_rows, key_ids):
    logit_entries = lax.dot_general(
        query_rows, key_rows, (((1,), (1,)), ((), ())), preferred_element_type=jnp.float32
    )
    similarity_grid = jnp.where(
        query_ids[:, None] == key_ids[None, :],
        jnp.exp((logit_entries - 1.0) / sharpness_divisor),
        jnp.zeros_like(logit_entries),
    )
    return (jnp.sum(similarity_grid, axis=1), jnp.sum(similarity_grid, axis=0))


def pair_sums(query_rows, query_ids, key_rows, key_ids):
    return dense_sums(query_rows, query_ids, key_rows, key_ids)


def body(embeddings, strata, centroids):
    own_units = unit_rows(embeddings[0])
    own_ids = strata[0]
    row_count = own_units.shape[0]
    cent_local = unit_rows(centroids[0])
    cent_units = lax.all_gather(cent_local, "blk", axis=0, tiled=True)
    strata_count = cent_units.shape[0]
    selector = (own_ids[:, None] == lax.broadcasted_iota(jnp.int32, (1, strata_count), 1)).astype(
        jnp.bfloat16
    )
    picked = jnp.dot(selector, cent_units, preferred_element_type=jnp.float32)
    distance = 1.0 - jnp.sum(own_units.astype(jnp.float32) * picked, axis=-1)
    guest_rows = lax.all_gather(own_units, "blk", axis=0, tiled=True)
    guest_ids = lax.all_gather(own_ids, "blk", axis=0, tiled=True)
    row_sums, column_sums = pair_sums(own_units, own_ids, guest_rows, guest_ids)
    weights = (distance + base_term) / row_sums
    total = lax.psum(jnp.sum(weights), ("blk", "grp"))
    row_total = float(row_count * lax.axis_size("blk") * lax.axis_size("grp"))
    return (weights * (row_total / total))[None, :]


def solution(mesh):
    placed = (P("grp", "blk", None), P("grp", "blk"), P("grp", "blk", None))
    return jax.shard_map(
        body, mesh=mesh, in_specs=placed, out_specs=P("grp", "blk"), check_vma=False
    )
```

profile of v0, /device:TPU:0, one launch (start us, length us, event | category | flops | bytes accessed | tf_op | source)
XLA Modules:
  0.0 197.1 jit_solution(4007569216989032687)
XLA Ops:
  6.5 0.0 all-gather.3.cloned.1.call-start
  6.5 1.5 fusion
  8.1 2.5 %fusion.1 = bf16[512,1024]{1,0:T(8,128)(2,1)} fusion(bf16[1,512,1024]{2,1,0:T(8,128)(2,1)} %param.3, f32[512]{0:T(512)S(1)} %rsqrt_multiply_fusion), kind=kLoop, calls=%fused_computation.4 | loop fusion | flops 1572864 | bytes 2099200 | tf_op jit(solution)/shard_map/convert_element_type | solution.py:17
  10.6 0.0 all-gather.3.cloned.1.call-update
  10.6 28.4 %all-gather = s32[1,4096]{1,0:T(1,128)S(1)} all-gather(s32[1,512]{1,0:T(1,128)} %param.4), channel_id=2, replica_groups=mesh['blk'=8,'grp'=4] {'blk'}, dimensions={1}, use_global_device_ids=true | all-gather | bytes 18432 | tf_op jit(solution)/shard_map/all_gather | solution.py:49
  39.0 0.9 fusion.3
  39.9 0.8 fusion.4
  40.7 31.6 %all_gather.9 = bf16[128,1024]{1,0:T(8,128)(2,1)S(1)} all-gather(bf16[16,1024]{1,0:T(8,128)(2,1)S(1)} %fusion.4), channel_id=1, replica_groups=mesh['blk'=8,'grp'=4] {'blk'}, dimensions={0}, use_global_device_ids=true | all-gather | bytes 294912 | tf_op jit(solution)/shard_map/all_gather | solution.py:41
  72.3 1.8 multiply_reduce_fusion
  74.1 66.4 %all-gather.3.cloned.1.call-done = bf16[4096,1024]{1,0:T(8,128)(2,1)} async-done(((bf16[512,1024]{1,0:T(8,128)(2,1)}), bf16[4096,1024]{1,0:T(8,128)(2,1)}) %all-gather.3.cloned.1.call-update) | async-done | bytes 8388624 | tf_op jit(solution)/shard_map/all_gather | solution.py:48
  140.5 9.1 %select_reduce_fusion = f32[512]{0:T(512)S(1)} fusion(bf16[512,1024]{1,0:T(8,128)(2,1)} %fusion.1, bf16[4096,1024]{1,0:T(8,128)(2,1)} %all-gather.3.cloned.1.call-done, s32[4096]{0:T(1024)S(1)} %bitcast.14, s32[512]{0:T(512)} %bitcast.16), kind=kOutput, calls=%fused_computation | convolution fusion | flops 4305452544 | bytes 9457664 | tf_op jit(solution)/shard_map/dot_general | solution.py:21
  149.6 0.6 fusion.5
  150.2 38.8 %psum.7 = f32[]{:T(128)} all-reduce(f32[]{:T(128)} %get-tuple-element.5), channel_id=1, replica_groups=mesh['blk'=8,'grp'=4] {'blk','grp'}, use_global_device_ids=true, to_apply=%region_5.6 | all-reduce | flops 1 | bytes 8 | tf_op jit(solution)/shard_map/psum | solution.py:52
  189.7 0.6 broadcast_multiply_fusion
  (2 shorter events, 0.0 us)
Async XLA Ops:
  6.5 134.0 %all-gather.3.cloned.1.call-start = ((), (), s32[]{:S(2)}) async-start(), calls=%async_computation | async-start | bytes 9437184 | tf_op jit(solution)/shard_map/all_gather | solution.py:48
Sparse Core Ops, SparseCore 0:
  10.7 129.7 all-gather.2
where the time goes:
time: 198 us; the launch traced here: 197 us
  blocking collectives  98.8 us (50%)
  waiting for transfers between devices  66.4 us (34%)
  between operations  14.1 us (7%)
  matrix products  10.9 us (6%)
  other arithmetic  6.97 us (4%)
    all_gather x1, waiting for transfers between devices, body(): guest_rows = lax.all_gather(own_units, 'blk', axis=0, tiled=True)  66.4 us
    psum x1, blocking collectives, body(): total = lax.psum(jnp.sum(weights), ('blk', 'grp'))  38.8 us
    all_gather x1, blocking collectives, body(): cent_units = lax.all_gather(cent_local, 'blk', axis=0, tiled=True)  31.6 us
    all_gather x1, blocking collectives, body(): guest_ids = lax.all_gather(own_ids, 'blk', axis=0, tiled=True)  28.4 us
    dot_general x1, matrix products, dense_sums(): lax.dot_general(query_rows, key_rows, (((1,), (1,)), ((), ())), preferred...  9.08 us
  transfers between devices with their start and end apart: 1, of which 1 were waited for; matrix products, arithmetic and copies ran while one was open for 2% of the time, Pallas kernels for 0%

commit v1 on v0

--- a/solution.py
+++ b/solution.py
@@ -46,7 +46,9 @@
     picked = jnp.dot(selector, cent_units, preferred_element_type=jnp.float32)
     distance = 1.0 - jnp.sum(own_units.astype(jnp.float32) * picked, axis=-1)
     guest_rows = lax.all_gather(own_units, "blk", axis=0, tiled=True)
-    guest_ids = lax.all_gather(own_ids, "blk", axis=0, tiled=True)
+    guest_ids = jnp.concatenate(
+        lax.all_to_all(jnp.stack([own_ids] * lax.axis_size("blk")), "blk", 0, 0), axis=0
+    )
     row_sums, column_sums = pair_sums(own_units, own_ids, guest_rows, guest_ids)
     weights = (distance + base_term) / row_sums
     total = lax.psum(jnp.sum(weights), ("blk", "grp"))

time: 198 us -> 198 us (level)
  blocking collectives: 98.8 us -> 71.3 us
  waiting for transfers between devices: 66.4 us -> 85.2 us
  starting transfers between devices: 0.01 us -> 7.28 us
    all_gather x1 -> x0, blocking collectives: 28.4 us -> none  [body(): guest_ids = lax.all_gather(own_ids, 'blk', axis=0, tiled=True)]
    all_gather x1, waiting for transfers between devices: 66.4 us -> 85.2 us  [body(): guest_rows = lax.all_gather(own_units, 'blk', axis=0, tiled=True)]
    all_to_all x0 -> x1, starting transfers between devices: none -> 7.28 us  [body(): lax.all_to_all(jnp.stack([own_ids] * lax.axis_size('blk')), 'blk', 0, 0)]
  transfers between devices with their start and end apart: 1 -> 2, of which waited for: 1 -> 1; matrix products, arithmetic and copies ran while one was open for 2% -> 2% of each run, Pallas kernels for 0% -> 0%
where the time goes in v1:
time: 198 us; the launch traced here: 197 us
  waiting for transfers between devices  85.2 us (43%)
  blocking collectives  71.3 us (36%)
  between operations  14.1 us (7%)
  matrix products  10.9 us (6%)
  starting transfers between devices  7.28 us (4%)
  other arithmetic  6.98 us (4%)
    all_gather x1, waiting for transfers between devices, body(): guest_rows = lax.all_gather(own_units, 'blk', axis=0, tiled=True)  85.2 us
    psum x1, blocking collectives, body(): total = lax.psum(jnp.sum(weights), ('blk', 'grp'))  38.6 us
    all_gather x1, blocking collectives, body(): cent_units = lax.all_gather(cent_local, 'blk', axis=0, tiled=True)  32.7 us
    dot_general x1, matrix products, dense_sums(): lax.dot_general(query_rows, key_rows, (((1,), (1,)), ((), ())), preferred...  9.08 us
    all_to_all x1, starting transfers between devices, body(): lax.all_to_all(jnp.stack([own_ids] * lax.axis_size('blk')), 'blk', 0, 0)  7.28 us
  transfers between devices with their start and end apart: 2, of which 1 were waited for; matrix products, arithmetic and copies ran while one was open for 2% of the time, Pallas kernels for 0%

profile of v1, /device:TPU:0, one launch (start us, length us, event | category | flops | bytes accessed | tf_op | source)
XLA Modules:
  0.0 197.1 jit_solution(4731645907116196583)
XLA Ops:
  6.5 0.0 all-gather.2.cloned.1.call-start
  6.5 1.5 fusion
  8.1 2.5 %fusion.1 = bf16[512,1024]{1,0:T(8,128)(2,1)} fusion(bf16[1,512,1024]{2,1,0:T(8,128)(2,1)} %param.3, f32[512]{0:T(512)S(1)} %rsqrt_multiply_fusion), kind=kLoop, calls=%fused_computation.4 | loop fusion | flops 1572864 | bytes 2099200 | tf_op jit(solution)/shard_map/convert_element_type | solution.py:17
  10.6 0.0 all-gather.2.cloned.1.call-update
  10.6 1.3 stack.3
  11.9 7.3 %all-to-all-start = ((s32[8,1,512]{2,1,0:T(1,128)}), s32[8,1,512]{2,1,0:T(1,128)S(1)}, u32[]{:S(2)}, u32[]{:S(2)}) async-start(s32[8,1,512]{2,1,0:T(1,128)} %stack.3), calls=%async_computation | async-start | bytes 32768 | tf_op jit(solution)/shard_map/all_to_all | solution.py:50
  19.2 0.9 fusion.3
  20.1 0.8 fusion.4
  20.9 32.7 %all_gather.6 = bf16[128,1024]{1,0:T(8,128)(2,1)S(1)} all-gather(bf16[16,1024]{1,0:T(8,128)(2,1)S(1)} %fusion.4), channel_id=1, replica_groups=mesh['blk'=8,'grp'=4] {'blk'}, dimensions={0}, use_global_device_ids=true | all-gather | bytes 294912 | tf_op jit(solution)/shard_map/all_gather | solution.py:41
  53.7 1.8 multiply_reduce_fusion
  55.5 0.0 all-to-all-done
  55.5 85.2 %all-gather.2.cloned.1.call-done = bf16[4096,1024]{1,0:T(8,128)(2,1)} async-done(((bf16[512,1024]{1,0:T(8,128)(2,1)}), bf16[4096,1024]{1,0:T(8,128)(2,1)}) %all-gather.2.cloned.1.call-update) | async-done | bytes 8388624 | tf_op jit(solution)/shard_map/all_gather | solution.py:48
  140.6 9.1 %select_reduce_fusion = f32[512]{0:T(512)S(1)} fusion(bf16[512,1024]{1,0:T(8,128)(2,1)} %fusion.1, bf16[4096,1024]{1,0:T(8,128)(2,1)} %all-gather.2.cloned.1.call-done, s32[4096]{0:T(1024)S(1)} %bitcast.14, s32[512]{0:T(512)} %bitcast.17), kind=kOutput, calls=%fused_computation | convolution fusion | flops 4305452544 | bytes 9457664 | tf_op jit(solution)/shard_map/dot_general | solution.py:21
  149.7 0.6 fusion.5
  150.3 38.6 %psum.7 = f32[]{:T(128)} all-reduce(f32[]{:T(128)} %get-tuple-element.5), channel_id=1, replica_groups=mesh['blk'=8,'grp'=4] {'blk','grp'}, use_global_device_ids=true, to_apply=%region_5.6 | all-reduce | flops 1 | bytes 8 | tf_op jit(solution)/shard_map/psum | solution.py:54
  189.6 0.6 broadcast_multiply_fusion
  (2 shorter events, 0.0 us)
Async XLA Ops:
  6.5 134.1 %all-gather.2.cloned.1.call-start = ((), (), s32[]{:S(2)}) async-start(), calls=%async_computation.1 | async-start | bytes 9437184 | tf_op jit(solution)/shard_map/all_gather | solution.py:48
  11.9 43.6 %all-to-all-start = ((s32[8,1,512]{2,1,0:T(1,128)}), s32[8,1,512]{2,1,0:T(1,128)S(1)}, u32[]{:S(2)}, u32[]{:S(2)}) async-start(s32[8,1,512]{2,1,0:T(1,128)} %stack.3), calls=%async_computation | async-start | bytes 32768 | tf_op jit(solution)/shard_map/all_to_all | solution.py:50
Sparse Core Ops, SparseCore 0:
  10.7 129.8 all-gather.1
